TPU v7x, 32 devices: a whole 2x2x4 slice. The times are simulated.
32 devices in a mesh: tile: 8 (over z, y), member: 4 (over x, core).
Axes of the slice: x: 2, y: 2, z: 4, core: 2. Of those that a mesh axis runs over, the one named last changes fastest.
Arguments:
- states: bfloat16 [4, 2048, 512], P('member', 'tile'), may hold values from -105 to 105
- teacher: bfloat16 [2048, 512], P('tile'), may hold values from -6 to 6
- w_qkv: bfloat16 [512, 1536], replicated, may hold values from -0.25 to 0.25
- w_out: bfloat16 [512, 512], replicated, may hold values from -0.25 to 0.25
- gain: float32 [512], replicated, may hold values from 0.1 to 1.9
- bias: float32 [8, 64, 64], replicated, may hold values from -4 to 400
- neighbours: int32 [32, 9], P('tile'), may hold values from 0 to 31, as said below
- valid: int32 [32, 9], P('tile'), may hold values from 0 to 1, as said below
- orient: int32 [32, 9], P('tile'), may hold values from 0 to 3, as said below
Outputs:
- output: bfloat16 [4, 2048, 512], P('member', 'tile')
- d_states: bfloat16 [4, 2048, 512], P('member', 'tile')
- d_wqkv: float32 [512, 1536], P('tile', 'member')
- d_wout: float32 [512, 512], P('tile', 'member')
- d_gain: float32 [512], replicated
- d_bias: float32 [8, 64, 64], replicated
Inputs may be any that keep to these rules, and one draw needn't show every extreme that they name: `neighbours`: for a block in column c, slots 3 m, 3 m + 1 and 3 m + 2 name blocks of column c + m - 1, block = column * 4 + row; where c + m - 1 lies outside 0 to 8 - 1 (the window's open ends) these slots name the block itself; slot 4 names the block itself. `valid`: slot 4 is always 1; slots whose column lies outside the window are 0. `orient`: slot 4 is always 0.
All inputs are finite; a program needn't handle non-finite values.
Results may differ from a plain program's by a relative error of at most 0.008.
Values may be sent and summed in bfloat16 or wider, within the bound.
No kernel may reach another device: no remote copies, remote signals or barrier semaphores. Data moves between devices by JAX's collectives and lax.ppermute only.
A program may use at most 128 MiB of HBM per device.

v0:
```python
import jax
import jax.numpy as jnp
from jax import lax
from jax.sharding import PartitionSpec as P

D = 512
HEADS = 8
HD = 64
SIDE = 8
PIX = 64
ROWS = 4
SLOTS = 9
COL_DEV = 1


EPS = 1e-06
NEG = -1e30
HIGH = lax.Precision.HIGHEST


def extended_2(cells, sides, width):
    for axis, dim in sides:
        count = lax.axis_size(axis)
        ends = count - 1
        head = lax.slice_in_dim(cells, 0, width, axis=dim)
        tail = lax.slice_in_dim(cells, cells.shape[dim] - width, cells.shape[dim], axis=dim)
        cells = jnp.concatenate(
            [
                lax.ppermute(tail, axis, [(i, (i + 1) % count) for i in range(ends)]),
                cells,
                lax.ppermute(head, axis, [((i + 1) % count, i) for i in range(ends)]),
            ],
            axis=dim,
        )
    return cells


def passed_along(value, axis, by):
    count = lax.axis_size(axis)
    pairs = [(i, i + by) for i in range(count) if 0 <= i + by < count]
    return lax.ppermute(value, axis, pairs)


def turn_onehot():
    position = jnp.arange(PIX, dtype=jnp.int32)
    upper = position // SIDE
    lower = position % SIDE
    tables = []
    for turn in range(4):
        tables.append(upper * SIDE + lower)
        upper, lower = (lower, SIDE - 1 - upper)
    table = jnp.stack(tables)
    return (table[:, :, None] == position[None, None, :]).astype(jnp.float32)


def probabilities(queries, keys_flat, inside, expander, turned_flat):
    scores = jnp.einsum(
        "gihd,gnhd->ghin", queries, keys_flat, preferred_element_type=jnp.float32
    ) * HD ** (-0.5)
    scores = scores + jnp.einsum("hic,gcn->ghin", turned_flat, expander, precision=HIGH)
    masked = jnp.where(inside, scores, NEG)
    highest = jnp.max(masked, axis=3, keepdims=True)
    weights = jnp.where(inside, jnp.exp(masked - highest), 0.0)
    return weights / jnp.sum(weights, axis=3, keepdims=True)


def shards(states, teacher, w_qkv, w_out, gain, bias, neighbours, valid, orient):
    inputs = states[0]
    n_rows = inputs.shape[0]
    blocks_here = neighbours.shape[0]
    cols_here = blocks_here // ROWS
    extended = blocks_here + 2 * ROWS
    rim_rows = ROWS * PIX
    n_tile = lax.axis_size("tile")
    n_member = lax.axis_size("member")
    first_column = lax.axis_index("tile") * COL_DEV
    columns_all = COL_DEV * n_tile
    near_column = jnp.mod(neighbours // ROWS - first_column + 1, columns_all)
    near_local = near_column * ROWS + neighbours % ROWS
    alive_flat = jnp.repeat(valid > 0, PIX, axis=1)
    inside = alive_flat[:, None, None, :]
    turn_pick = (orient[:, :, None] == jnp.arange(4, dtype=jnp.int32)[None, None, :]).astype(
        jnp.float32
    )
    identity = jnp.eye(PIX, dtype=jnp.float32)
    expander = jnp.einsum("gsk,jl->gkjsl", turn_pick, identity, precision=HIGH).reshape(
        blocks_here, 4 * PIX, SLOTS * PIX
    )
    onehot_turn = turn_onehot()
    turned = jnp.einsum("ail,kjl->kaij", bias, onehot_turn, precision=HIGH)
    turned_flat = jnp.transpose(turned, (1, 2, 0, 3)).reshape(HEADS, PIX, 4 * PIX)
    inputs32 = inputs.astype(jnp.float32)
    inverse = lax.rsqrt(jnp.mean(inputs32 * inputs32, axis=-1, keepdims=True) + EPS)
    normed = (inputs32 * inverse * gain).astype(jnp.bfloat16)
    projected = jnp.dot(normed, w_qkv, preferred_element_type=jnp.float32).astype(jnp.bfloat16)
    queries = projected[:, :D].reshape(blocks_here, PIX, HEADS, HD)
    keyval = projected[:, D:]
    keyval_ext = extended_2(keyval, (("tile", 0),), rim_rows)
    keyval_near = jnp.take(keyval_ext.reshape(extended, PIX, 2 * D), near_local, axis=0)
    keys_flat = keyval_near[..., :D].reshape(blocks_here, SLOTS * PIX, HEADS, HD)
    values_flat = keyval_near[..., D:].reshape(blocks_here, SLOTS * PIX, HEADS, HD)
    probs = probabilities(queries, keys_flat, inside, expander, turned_flat)
    probs_low = probs.astype(jnp.bfloat16)
    mixed = jnp.einsum(
        "ghin,gnhd->gihd", probs_low, values_flat, preferred_element_type=jnp.float32
    )
    mixed = mixed.astype(jnp.bfloat16).reshape(n_rows, D)
    output32 = inputs32 + jnp.dot(mixed, w_out, preferred_element_type=jnp.float32)
    d_output = (output32 - teacher.astype(jnp.float32)).astype(jnp.bfloat16)
    d_mixed = jnp.dot(d_output, w_out.T, preferred_element_type=jnp.float32).astype(jnp.bfloat16)
    d_mixed = d_mixed.reshape(blocks_here, PIX, HEADS, HD)
    d_probs = jnp.einsum(
        "gihd,gnhd->ghin", d_mixed, values_flat, preferred_element_type=jnp.float32
    )
    delta_sum = jnp.sum(probs * d_probs, axis=3, keepdims=True)
    d_scores = probs * (d_probs - delta_sum)
    d_scores_low = d_scores.astype(jnp.bfloat16)
    d_queries = jnp.einsum(
        "ghin,gnhd->gihd", d_scores_low, keys_flat, preferred_element_type=jnp.float32
    ) * HD ** (-0.5)
    d_queries = d_queries.astype(jnp.bfloat16).reshape(n_rows, D)
    d_keys = jnp.einsum(
        "ghin,gihd->gnhd", d_scores_low, queries, preferred_element_type=jnp.float32
    ) * HD ** (-0.5)
    d_values = jnp.einsum("ghin,gihd->gnhd", probs_low, d_mixed, preferred_element_type=jnp.float32)
    d_near = jnp.concatenate(
        [
            d_keys.reshape(blocks_here * SLOTS, PIX, D),
            d_values.reshape(blocks_here * SLOTS, PIX, D),
        ],
        axis=-1,
    )
    d_near = d_near.reshape(cols_here, ROWS, 3, 3, PIX * 2 * D)
    target_row = (neighbours % ROWS).reshape(cols_here, ROWS, 3, 3)
    row_onehot = (target_row[..., None] == jnp.arange(ROWS, dtype=jnp.int32)).astype(jnp.float32)
    per_group = jnp.einsum("cqmkt,cqmkx->mctx", row_onehot, d_near, precision=HIGH)
    d_columns = jnp.pad(per_group[0], ((0, 2), (0, 0), (0, 0)))
    d_columns = d_columns + jnp.pad(per_group[1], ((1, 1), (0, 0), (0, 0)))
    d_columns = d_columns + jnp.pad(per_group[2], ((2, 0), (0, 0), (0, 0)))
    d_extended = d_columns.reshape(extended * PIX, 2 * D)
    from_right = passed_along(d_extended[:rim_rows].astype(jnp.bfloat16), "tile", -1).astype(
        jnp.float32
    )
    from_left = passed_along(
        d_extended[extended * PIX - rim_rows :].astype(jnp.bfloat16), "tile", 1
    ).astype(jnp.float32)
    d_keyval = d_extended[rim_rows : extended * PIX - rim_rows]
    d_keyval = d_keyval.at[:rim_rows].add(from_left)
    d_keyval = d_keyval.at[n_rows - rim_rows :].add(from_right)
    d_proj = jnp.concatenate([d_queries, d_keyval.astype(jnp.bfloat16)], axis=-1)
    d_normed = jnp.dot(d_proj, w_qkv.T, preferred_element_type=jnp.float32)
    gain_term = jnp.sum(d_normed * inputs32 * inverse, axis=0)
    d_scaled = d_normed * gain
    d_inputs = (
        d_output.astype(jnp.float32)
        + inverse * d_scaled
        - inputs32
        * inverse
        * inverse
        * inverse
        * jnp.mean(d_scaled * inputs32, axis=-1, keepdims=True)
    )
    d_table = jnp.einsum("ghin,gcn->hic", d_scores, expander, precision=HIGH)
    d_turned = jnp.transpose(d_table.reshape(HEADS, PIX, 4, PIX), (2, 0, 1, 3))
    bias_term = jnp.einsum("khij,kjl->hil", d_turned, onehot_turn, precision=HIGH)
    gain_total, bias_total = lax.psum((gain_term, bias_term), ("tile", "member"))
    proj_cols = 3 * D // n_member
    out_cols = D // n_member
    proj_part = jnp.einsum("rd,re->de", normed, d_proj, preferred_element_type=jnp.float32).reshape(
        D, n_member, proj_cols
    )
    out_part = jnp.einsum("rd,re->de", mixed, d_output, preferred_element_type=jnp.float32).reshape(
        D, n_member, out_cols
    )
    whole_term = jnp.concatenate([proj_part, out_part], axis=2)
    member_shares = lax.psum_scatter(
        whole_term.astype(jnp.bfloat16), "member", scatter_dimension=1, tiled=True
    ).astype(jnp.float32)
    summed = lax.psum_scatter(member_shares, "tile", scatter_dimension=0, tiled=True)
    d_wqkv = summed[:, 0, :proj_cols]
    d_wout = summed[:, 0, proj_cols:]
    return (
        output32.astype(jnp.bfloat16)[None],
        d_inputs.astype(jnp.bfloat16)[None],
        d_wqkv,
        d_wout,
        gain_total,
        bias_total,
    )


def solution(mesh):
    return jax.shard_map(
        shards,
        mesh=mesh,
        in_specs=(
            P("member", "tile", None),
            P("tile", None),
            P(),
            P(),
            P(),
            P(),
            P("tile", None),
            P("tile", None),
            P("tile", None),
        ),
        out_specs=(
            P("member", "tile", None),
            P("member", "tile", None),
            P("tile", "member"),
            P("tile", "member"),
            P(),
            P(),
        ),
        check_vma=False,
    )
```

profile of v0, /device:TPU:0, one launch (start us, length us, event | category | flops | bytes accessed | tf_op | source)
XLA Modules:
  0.0 496.8 jit_solution(8968497430572609303)
XLA Ops:
  11.6 6.4 %collective-permute-start = (bf16[256,1024]{1,0:T(8,128)(2,1)S(1)}, bf16[256,1024]{1,0:T(8,128)(2,1)}, u32[]{:S(2)}, u32[]{:S(2)}) collective-permute-start(bf16[256,1024]{1,0:T(8,128)(2,1)S(1)} %slice.87), channel_id=1, source_target_pairs={{0,4},{4,8},{8,12},{12,16},{16,20},{20,24},{24,28},{1,5},{5,9},{9,... | collective-permute-start | bytes 1572872 | tf_op jit(solution)/shard_map/ppermute | solution.py:29
  27.9 5.9 %reshape.271 = f32[4,256,576,1]{1,2,0,3:T(8,128)} reshape(f32[4,4,64,9,64]{2,1,4,3,0:T(4,128)} %multiply_bitcast_fusion.1) | data formatting | bytes 4718592 | tf_op jit(solution)/shard_map/reshape | solution.py:86
  50.2 7.0 %reshape.249 = bf16[4,576,8,64]{3,2,1,0:T(8,128)(2,1)} reshape(bf16[4,9,64,512]{3,2,1,0:T(8,128)(2,1)} %get-tuple-element.72) | data formatting | bytes 4718592 | tf_op jit(solution)/shard_map/reshape | solution.py:100
  57.2 6.2 %copy.68 = bf16[4,576,8,64]{1,3,2,0:T(8,128)(2,1)} copy(bf16[4,576,8,64]{3,2,1,0:T(8,128)(2,1)} %reshape.249) | data formatting | bytes 4718592 | tf_op jit(solution)/shard_map/reshape | solution.py:100
  63.4 7.0 %reshape.247 = bf16[4,576,8,64]{3,2,1,0:T(8,128)(2,1)} reshape(bf16[4,9,64,512]{3,2,1,0:T(8,128)(2,1)} %get-tuple-element.73) | data formatting | bytes 4718592 | tf_op jit(solution)/shard_map/reshape | solution.py:101
  70.5 6.3 %copy.70 = bf16[4,576,8,64]{1,3,2,0:T(8,128)(2,1)} copy(bf16[4,576,8,64]{3,2,1,0:T(8,128)(2,1)} %reshape.247) | data formatting | bytes 4718592 | tf_op jit(solution)/shard_map/reshape | solution.py:101
  79.6 5.5 %fusion.4 = f32[4,8,64,576]{3,2,1,0:T(8,128)S(1)} fusion(f32[4,8,64,576]{3,2,1,0:T(8,128)S(1)} %fusion.75, pred[4,576]{1,0:T(4,128)(4,1)S(1)} %broadcast_in_dim.57, f32[8,64,256,1]{2,1,0,3:T(8,128)S(1)} %copy-done.11, f32[4,256,576,1]{1,2,0,3:T(8,128)S(1)} %copy-done.3), kind=kOutput, calls=%fused_computation.8 | convolution fusion | flops 3627417600 | bytes 12323072 | tf_op jit(solution)/shard_map/hic,gcn->ghin/dot_general | solution.py:60
  100.7 7.0 %multiply_reduce_fusion = (f32[4,8,64]{2,1,0:T(8,128)S(1)}, f32[4,8,64,576]{3,2,1,0:T(8,128)}) fusion(f32[4,8,64,576]{3,2,1,0:T(8,128)} %copy-done.2, f32[4,8,64]{2,1,0:T(8,128)S(1)} %get-tuple-element.80, bf16[4,64,8,64]{1,3,2,0:T(8,128)(2,1)} %copy.79, bf16[4,576,8,64]{1,3,2,0:T(8,128)(2,1)} %copy.70), kind=kOutput, calls=%fused_computation.11 | convolution fusion | flops 154531840 | bytes 12075008 | tf_op jit(solution)/shard_map/gihd,gnhd->ghin/dot_general | solution.py:112
  112.8 8.1 %copy.80 = f32[4,576,8,64]{3,2,1,0:T(8,128)} copy(f32[4,576,8,64]{1,3,2,0:T(8,128)} %convolution_bitcast_fusion.1) | data formatting | bytes 9437184 | tf_op jit(solution)/shard_map/ghin,gihd->gnhd/transpose | solution.py:125
  121.0 8.9 %reshape.256 = f32[36,64,512]{2,1,0:T(8,128)} reshape(f32[4,576,8,64]{3,2,1,0:T(8,128)} %copy.80) | data formatting | bytes 9437184 | tf_op jit(solution)/shard_map/reshape | solution.py:129
  129.9 6.2 %fusion.8 = (f32[4,8,64,576,1]{3,2,1,0,4:T(8,128)}, bf16[4,8,64,576]{3,2,1,0:T(8,128)(2,1)S(1)}) fusion(f32[4,8,64,576]{3,2,1,0:T(8,128)} %get-tuple-element.83, f32[4,8,64]{2,1,0:T(8,128)S(1)} %get-tuple-element.82, f32[4,8,64,576]{3,2,1,0:T(8,128)} %copy-done.2, f32[4,8,64]{2,1,0:T(8,128)S(1)} %get-tuple-element.80), kind=kLoop, calls=%fused_computation.23 | loop fusion | flops 4718592 | bytes 16531456 | tf_op jit(solution)/shard_map/mul | solution.py:116
  140.8 8.1 %copy.78 = f32[4,576,8,64]{3,2,1,0:T(8,128)} copy(f32[4,576,8,64]{1,3,2,0:T(8,128)} %multiply_bitcast_fusion) | data formatting | bytes 9437184 | tf_op jit(solution)/shard_map/mul | solution.py:122
  148.9 8.9 %reshape.255 = f32[36,64,512]{2,1,0:T(8,128)} reshape(f32[4,576,8,64]{3,2,1,0:T(8,128)} %copy.78) | data formatting | bytes 9437184 | tf_op jit(solution)/shard_map/reshape | solution.py:128
  157.9 9.1 %pad_maximum_fusion = f32[36,64,1024]{2,1,0:T(8,128)} fusion(f32[36,64,512]{2,1,0:T(8,128)} %reshape.256, f32[36,64,512]{2,1,0:T(8,128)} %reshape.255), kind=kLoop, calls=%fused_computation.3 | loop fusion | flops 2359296 | bytes 18874368 | tf_op jit(solution)/shard_map/concatenate | solution.py:126
  166.9 14.0 %reshape.257 = f32[4,3,3,65536]{3,2,1,0:T(4,128)} reshape(f32[36,64,1024]{2,1,0:T(8,128)} %pad_maximum_fusion) | data formatting | bytes 18874368 | tf_op jit(solution)/shard_map/reshape.68
  181.0 20.5 %convolution_bitcast_fusion = f32[3,4,65536]{2,1,0:T(4,128)S(1)} fusion(f32[4,3,3,65536]{3,2,1,0:T(4,128)} %reshape.257, s32[4,3,3]{0,2,1:T(4,128)S(1)} %copy.76), kind=kOutput, calls=%fused_computation.2 | convolution fusion | flops 113246352 | bytes 12583056 | tf_op jit(solution)/shard_map/cqmkt,cqmkx->mctx/dot_general | solution.py:136
  209.1 6.1 %collective-permute-start.2 = (bf16[256,1024]{1,0:T(8,128)(2,1)}, bf16[256,1024]{1,0:T(8,128)(2,1)}, u32[]{:S(2)}, u32[]{:S(2)}) collective-permute-start(bf16[256,1024]{1,0:T(8,128)(2,1)} %convert_element_type.102), channel_id=1, source_target_pairs={{0,4},{4,8},{8,12},{12,16},{16,20},{20,24},{24,28},{1,5},{5,9},{9,... | collective-permute-start | bytes 1572872 | tf_op jit(solution)/shard_map/ppermute | solution.py:41
  225.5 10.6 %collective-permute-done.2 = bf16[256,1024]{1,0:T(8,128)(2,1)} collective-permute-done((bf16[256,1024]{1,0:T(8,128)(2,1)}, bf16[256,1024]{1,0:T(8,128)(2,1)}, u32[]{:S(2)}, u32[]{:S(2)}) %collective-permute-start.2) | collective-permute-done | bytes 524320 | tf_op jit(solution)/shard_map/ppermute | solution.py:41
  241.9 32.5 %reduce-scatter.2.cloned.1.call-done = bf16[512,1,512]{0,2,1:T(8,128)(2,1)} async-done(((bf16[512,4,512]{0,2,1:T(8,128)(2,1)}), bf16[512,1,512]{0,2,1:T(8,128)(2,1)}) %reduce-scatter.2.cloned.1.call-update) | async-done | bytes 524304 | tf_op jit(solution)/shard_map/reduce_scatter | solution.py:176
  277.9 5.4 %reshape.250 = f32[4,256,576]{1,2,0:T(8,128)} reshape(f32[4,4,64,9,64]{2,1,4,3,0:T(4,128)} %multiply_bitcast_fusion.1) | data formatting | bytes 4718592 | tf_op jit(solution)/shard_map/reshape | solution.py:86
  287.8 10.7 %fusion.10 = f32[4,8,64,64]{3,2,0,1:T(8,128)S(1)} fusion(f32[4,64,4,576]{3,1,0,2:T(8,128)} %bitcast.155, f32[4,8,64,576,1]{3,2,1,0,4:T(8,128)} %get-tuple-element.70), kind=kOutput, calls=%fused_computation.27 | convolution fusion | flops 3623878656 | bytes 7602176 | tf_op jit(solution)/shard_map/ghin,gcn->hic/dot_general | solution.py:163
  300.7 39.6 %psum.14 = f32[512]{0:T(512)} all-reduce(f32[512]{0:T(512)S(1)} %get-tuple-element.64), channel_id=1, replica_groups=mesh['tile'=8,'member'=4] {'tile','member'}, use_global_device_ids=true, to_apply=%region_8.9 | all-reduce | flops 512 | bytes 4096 | tf_op jit(solution)/shard_map/psum | solution.py:166
  341.2 15.3 %all-reduce.8.cloned.1.call-done = f32[512,1,512]{2,1,0:T(1,128)} async-done(((f32[512,1,512]{2,1,0:T(1,128)}), f32[512,1,512]{2,1,0:T(1,128)}) %all-reduce.8.cloned.1.call-update) | async-done | bytes 1048592
  359.6 128.6 %all-reduce.6.cloned.1.call-done = f32[8,64,64]{2,1,0:T(8,128)} async-done(((f32[8,64,64]{2,1,0:T(8,128)}), f32[8,64,64]{2,1,0:T(8,128)}) %all-reduce.6.cloned.1.call-update) | async-done | bytes 131088 | tf_op jit(solution)/shard_map/psum | solution.py:166
  (137 shorter events, 97.4 us)
Async XLA Ops:
  7.2 10.8 %copy-start.23 = (s32[4,9]{1,0:T(4,128)S(1)}, s32[4,9]{1,0:T(4,128)}, u32[]{:S(2)}) copy-start(s32[4,9]{1,0:T(4,128)} %param.24) | copy-start | bytes 436
  7.2 10.8 %copy-start.21 = (s32[4,9]{1,0:T(4,128)S(1)}, s32[4,9]{1,0:T(4,128)}, u32[]{:S(2)}) copy-start(s32[4,9]{1,0:T(4,128)} %param.23) | copy-start | bytes 436
  7.2 11.3 %copy-start.22 = (s32[4,9]{1,0:T(4,128)S(1)}, s32[4,9]{1,0:T(4,128)}, u32[]{:S(2)}) copy-start(s32[4,9]{1,0:T(4,128)} %param.25) | copy-start | bytes 436
  7.2 12.8 %copy-start.19 = (f32[8,64,64]{2,1,0:T(8,128)S(1)}, f32[8,64,64]{2,1,0:T(8,128)}, u32[]{:S(2)}) copy-start(f32[8,64,64]{2,1,0:T(8,128)} %param.22) | copy-start | bytes 393220
  7.2 267.1 %reduce-scatter.2.cloned.1.call-start = ((), (), s32[]{:S(2)}) async-start(), calls=%async_computation.1 | async-start | bytes 2621440 | tf_op jit(solution)/shard_map/reduce_scatter | solution.py:176
  10.3 14.4 %copy-start.13 = (bf16[256,1024]{1,0:T(8,128)(2,1)}, bf16[256,1024]{1,0:T(8,128)(2,1)S(1)}, u32[]{:S(2)}) copy-start(bf16[256,1024]{1,0:T(8,128)(2,1)S(1)} %slice.87) | copy-start | bytes 1572868
  10.3 23.5 %collective-permute-start.1 = (bf16[256,1024]{1,0:T(8,128)(2,1)S(1)}, bf16[256,1024]{1,0:T(8,128)(2,1)}, u32[]{:S(2)}, u32[]{:S(2)}) collective-permute-start(bf16[256,1024]{1,0:T(8,128)(2,1)S(1)} %slice.87), channel_id=1, source_target_pairs={{4,0},{8,4},{12,8},{16,12},{20,16},{24,20},{28,24},{5,1},{9,5},{13... | collective-permute-start | bytes 1572872 | tf_op jit(solution)/shard_map/ppermute | solution.py:31
  11.6 26.9 %collective-permute-start = (bf16[256,1024]{1,0:T(8,128)(2,1)S(1)}, bf16[256,1024]{1,0:T(8,128)(2,1)}, u32[]{:S(2)}, u32[]{:S(2)}) collective-permute-start(bf16[256,1024]{1,0:T(8,128)(2,1)S(1)} %slice.87), channel_id=1, source_target_pairs={{0,4},{4,8},{8,12},{12,16},{16,20},{20,24},{24,28},{1,5},{5,9},{9,... | collective-permute-start | bytes 1572872 | tf_op jit(solution)/shard_map/ppermute | solution.py:29
  70.5 6.3 %copy-start.4 = (bf16[4,64,8,64]{1,3,2,0:T(8,128)(2,1)S(1)}, bf16[4,64,8,64]{1,3,2,0:T(8,128)(2,1)}, u32[]{:S(2)}) copy-start(bf16[4,64,8,64]{1,3,2,0:T(8,128)(2,1)} %copy.77) | copy-start | bytes 786436
  89.1 5.3 %copy-start.12 = (bf16[512,512]{1,0:T(8,128)(2,1)S(1)}, bf16[512,512]{1,0:T(8,128)(2,1)}, u32[]{:S(2)}) copy-start(bf16[512,512]{1,0:T(8,128)(2,1)} %param.20) | copy-start | bytes 1572868
  98.5 9.3 %slice-start = ((s8[5242880]{0:T(1024)(128)(4,1)}), s8[1048576]{0:T(1024)(128)(4,1)S(1)}, s32[]{:S(2)}) async-start(s8[5242880]{0:T(1024)(128)(4,1)} %bitcast.149), calls=%async_computation.4 | async-start | bytes 2097152
  100.7 7.1 %slice-start.1 = ((s8[5242880]{0:T(1024)(128)(4,1)}), s8[4194304]{0:T(1024)(128)(4,1)S(1)}, s32[]{:S(2)}) async-start(s8[5242880]{0:T(1024)(128)(4,1)} %bitcast.149), calls=%async_computation.5 | async-start | bytes 8388608
  100.7 7.1 %copy-start.18 = (bf16[4,64,8,64]{1,3,2,0:T(8,128)(2,1)S(1)}, bf16[4,64,8,64]{1,3,2,0:T(8,128)(2,1)}, u32[]{:S(2)}) copy-start(bf16[4,64,8,64]{1,3,2,0:T(8,128)(2,1)} %copy.79) | copy-start | bytes 786436
  207.8 17.7 %collective-permute-start.3 = (bf16[256,1024]{1,0:T(8,128)(2,1)}, bf16[256,1024]{1,0:T(8,128)(2,1)}, u32[]{:S(2)}, u32[]{:S(2)}) collective-permute-start(bf16[256,1024]{1,0:T(8,128)(2,1)} %convert_element_type.104), channel_id=1, source_target_pairs={{4,0},{8,4},{12,8},{16,12},{20,16},{24,20},{28,24},{5,1},{9,5},{13... | collective-permute-start | bytes 1572872 | tf_op jit(solution)/shard_map/ppermute | solution.py:41
  209.1 27.0 %collective-permute-start.2 = (bf16[256,1024]{1,0:T(8,128)(2,1)}, bf16[256,1024]{1,0:T(8,128)(2,1)}, u32[]{:S(2)}, u32[]{:S(2)}) collective-permute-start(bf16[256,1024]{1,0:T(8,128)(2,1)} %convert_element_type.102), channel_id=1, source_target_pairs={{0,4},{4,8},{8,12},{12,16},{16,20},{20,24},{24,28},{1,5},{5,9},{9,... | collective-permute-start | bytes 1572872 | tf_op jit(solution)/shard_map/ppermute | solution.py:41
  218.7 5.6 %copy-start.16 = (bf16[256,512,1]{1,0,2:T(8,128)(2,1)S(1)}, bf16[256,512,1]{1,0,2:T(8,128)(2,1)}, u32[]{:S(2)}) copy-start(bf16[256,512,1]{1,0,2:T(8,128)(2,1)} %reshape.275) | copy-start | bytes 786436
  218.8 5.6 %copy-start.17 = (bf16[512,256]{1,0:T(8,128)(2,1)S(1)}, bf16[512,256]{1,0:T(8,128)(2,1)}, u32[]{:S(2)}) copy-start(bf16[512,256]{1,0:T(8,128)(2,1)} %copy.94) | copy-start | bytes 786436
  224.3 14.0 %copy-start.14 = (bf16[256,512]{1,0:T(8,128)(2,1)S(1)}, bf16[256,512]{1,0:T(8,128)(2,1)}, u32[]{:S(2)}) copy-start(bf16[256,512]{1,0:T(8,128)(2,1)} %reshape.254) | copy-start | bytes 786436
  225.5 13.2 %copy-start.20 = (f32[512]{0:T(512)S(1)}, f32[512]{0:T(512)}, u32[]{:S(2)}) copy-start(f32[512]{0:T(512)} %param.21) | copy-start | bytes 6148
  241.9 114.7 %all-reduce.8.cloned.1.call-start = ((), (), s32[]{:S(2)}) async-start(), calls=%async_computation.3 | async-start | bytes 2097152
  277.8 210.4 %all-reduce.6.cloned.1.call-start = ((), (), s32[]{:S(2)}) async-start(), calls=%async_computation.2 | async-start | bytes 524288 | tf_op jit(solution)/shard_map/psum | solution.py:166
  287.7 12.1 %copy-start.10 = (bf16[256,1024]{1,0:T(8,128)(2,1)S(1)}, bf16[256,1024]{1,0:T(8,128)(2,1)}, u32[]{:S(2)}) copy-start(bf16[256,1024]{1,0:T(8,128)(2,1)} %copy-done.9) | copy-start | bytes 1572868
  287.8 12.1 %copy-start.15 = (bf16[256,512]{1,0:T(8,128)(2,1)S(1)}, bf16[256,512]{1,0:T(8,128)(2,1)}, u32[]{:S(2)}) copy-start(bf16[256,512]{1,0:T(8,128)(2,1)} %reshape.254) | copy-start | bytes 786436
  298.5 41.8 %copy-start.7 = (bf16[256,512]{1,0:T(8,128)(2,1)S(1)}, bf16[256,512]{1,0:T(8,128)(2,1)}, u32[]{:S(2)}) copy-start(bf16[256,512]{1,0:T(8,128)(2,1)} %copy-done.6) | copy-start | bytes 786436
  (11 other events, 25.5 us)
Sparse Core Ops, SparseCore 0:
  242.0 32.3 reduce-scatter.1
  277.9 78.5 all-reduce.7
  362.0 126.1 all-reduce.5
where the time goes:
time: 503 us; the launch traced here: 497 us
  waiting for transfers between devices  192 us (38%)
  local copies, waits for them, and re-layouts  135 us (27%)
  matrix products  66.7 us (13%)
  blocking collectives  39.6 us (8%)
  other arithmetic  33.7 us (7%)
  between operations  15.3 us (3%)
  starting transfers between devices  15.2 us (3%)
    psum x1, waiting for transfers between devices, shards(): lax.psum((gain_term, bias_term), ('tile', 'member'))  129 us
    psum x1, blocking collectives, shards(): lax.psum((gain_term, bias_term), ('tile', 'member'))  39.6 us
    reduce_scatter x1, waiting for transfers between devices, shards(): lax.psum_scatter(whole_term.astype(jnp.bfloat16), 'member', scatter_dimen...  32.5 us
    dot_general x1, matrix products, shards(): jnp.einsum('cqmkt,cqmkx->mctx', row_onehot, d_near, precision=HIGH)  20.5 us
    unnamed x4, waiting for transfers between devices  15.3 us
    another operation x1, local copies, waits for them, and re-layouts  14 us
    reshape x2, local copies, waits for them, and re-layouts, shards(): keyval_near[..., D:].reshape(blocks_here, SLOTS * PIX, HEADS, HD)  13.3 us
    reshape x2, local copies, waits for them, and re-layouts, shards(): keyval_near[..., :D].reshape(blocks_here, SLOTS * PIX, HEADS, HD)  13.3 us
  transfers between devices with their start and end apart: 7, of which 5 were waited for; matrix products, arithmetic and copies ran while one was open for 10% of the time, Pallas kernels for 0%

commit v1 on v0

v1 whole, which is shorter than its diff:
```python
import functools

import jax
import jax.numpy as jnp
from jax import lax
from jax.experimental import pallas as pl
from jax.experimental.pallas import tpu as pltpu
from jax.sharding import PartitionSpec as P

HD = 64
SIDE = 8
PIX = 64
ROWS = 4
SLOTS = 9
PAD_SLOTS = 10
PAIRS = PAD_SLOTS // 2
GROUP = 4
TURNS = 4
COL_DEV = 1

EPS = 1e-06
NEG = -1e30
HIGH = lax.Precision.HIGHEST
BF = jnp.bfloat16
F32 = jnp.float32

VM = pltpu.MemorySpace.VMEM
SM = pltpu.MemorySpace.SMEM


def nn(a, b):
    return jnp.dot(a, b, preferred_element_type=F32)


def nt(a, b):
    return lax.dot_general(a, b, (((1,), (1,)), ((), ())), preferred_element_type=F32)


def tn(a, b):
    return lax.dot_general(a, b, (((0,), (0,)), ((), ())), preferred_element_type=F32)


def turn_index(position, turn):
    upper = position // SIDE
    lower = position % SIDE
    for _ in range(turn):
        upper, lower = lower, SIDE - 1 - upper
    return upper * SIDE + lower


def rms(x32):
    return lax.rsqrt(jnp.mean(x32 * x32, axis=-1, keepdims=True) + EPS)


def own_kernel(x_ref, gain_ref, w_ref, bias_ref, normed_ref, proj_ref, table_ref):
    x32 = x_ref[...].astype(F32)
    normed = (x32 * rms(x32) * gain_ref[...]).astype(BF)
    normed_ref[...] = normed
    proj_ref[...] = nn(normed, w_ref[...]).astype(BF)
    source = lax.broadcasted_iota(jnp.int32, (PIX, 2 * PIX), 0)
    target = lax.broadcasted_iota(jnp.int32, (PIX, 2 * PIX), 1) & (PIX - 1)
    for turn in range(TURNS):
        pick = (turn_index(target, turn) == source).astype(F32)
        table_ref[turn] = jnp.dot(bias_ref[...], pick, preferred_element_type=F32, precision=HIGH)


def attention_kernel(
    near_ref, turn_ref, drop_ref,
    x_ref, xl_ref, xr_ref, proj_ref, table_ref, gain_ref, w_ref, wo_ref, teacher_ref,
    out_ref, dout_ref, mixed_ref, dq_ref, own_ref, left_ref, right_ref, bias_ref,
    kv, cat, prob, dmix, acc, tacc,
):
    dim = x_ref.shape[1]
    rows = x_ref.shape[0]
    blocks = rows // PIX
    groups = dim // (GROUP * HD)
    wide = GROUP * HD
    scale = HD ** -0.5
    head_of = lax.broadcasted_iota(jnp.int32, (PIX, wide), 1) // HD
    low_half = lax.broadcasted_iota(jnp.int32, (wide, 2 * PIX), 1) < PIX
    low_row = lax.broadcasted_iota(jnp.int32, (1, 2 * PIX), 1) < PIX

    def stacked(block):
        return jnp.concatenate(
            [jnp.where(head_of == h, block, 0.0) for h in range(GROUP)], axis=0
        ).astype(BF)

    def unstacked(tall):
        picked = tall[:PIX]
        for h in range(1, GROUP):
            picked = jnp.where(head_of == h, tall[h * PIX : (h + 1) * PIX], picked)
        return picked

    kv[rows : 2 * rows, :] = proj_ref[:, dim:]
    for side_ref, at in ((xl_ref, 0), (xr_ref, 2 * rows)):
        s32 = side_ref[...].astype(F32)
        normed = (s32 * rms(s32) * gain_ref[...]).astype(BF)
        kv[at : at + rows, :] = nn(normed, w_ref[:, dim:]).astype(BF)
    acc[...] = jnp.zeros_like(acc)
    tacc[...] = jnp.zeros_like(tacc)

    def forward(b, carry):
        for s in range(PAD_SLOTS):
            start = pl.multiple_of(near_ref[b * PAD_SLOTS + s] * PIX, PIX)
            cat[b, s * PIX : (s + 1) * PIX, :] = kv[pl.ds(start, PIX), :]
        base = pl.multiple_of(b * PIX, PIX)
        for g in range(groups):
            lanes = slice(g * wide, (g + 1) * wide)
            q = stacked(proj_ref[pl.ds(base, PIX), lanes].astype(F32) * scale)
            scores = nt(q, cat[b, :, lanes])
            parts = []
            for p in range(PAIRS):
                first = b * PAD_SLOTS + 2 * p
                low = table_ref[turn_ref[first], lanes, :]
                high = table_ref[turn_ref[first + 1], lanes, :]
                drop = jnp.where(low_row, drop_ref[first], drop_ref[first + 1])
                tile = scores[:, p * 2 * PIX : (p + 1) * 2 * PIX]
                parts.append(tile + jnp.where(low_half, low, high) + drop)
            full = jnp.concatenate(parts, axis=1)
            highest = jnp.max(full, axis=1, keepdims=True)
            weights = jnp.exp(full - highest)
            probs = weights * (1.0 / jnp.sum(weights, axis=1, keepdims=True))
            prob[b, lanes, :] = probs
            tall = nn(probs.astype(BF), cat[b, :, dim + g * wide : dim + (g + 1) * wide])
            mixed_ref[pl.ds(base, PIX), lanes] = unstacked(tall).astype(BF)
        return carry

    lax.fori_loop(0, blocks, forward, 0)

    out32 = x_ref[...].astype(F32) + nn(mixed_ref[...], wo_ref[...])
    out_ref[...] = out32.astype(BF)
    d_out = (out32 - teacher_ref[...].astype(F32)).astype(BF)
    dout_ref[...] = d_out
    dmix[...] = nt(d_out, wo_ref[...]).astype(BF)

    def backward(b, carry):
        base = pl.multiple_of(b * PIX, PIX)
        for g in range(groups):
            lanes = slice(g * wide, (g + 1) * wide)
            upper = slice(dim + g * wide, dim + (g + 1) * wide)
            q = stacked(proj_ref[pl.ds(base, PIX), lanes].astype(F32) * scale)
            dm = stacked(dmix[pl.ds(base, PIX), lanes].astype(F32))
            probs = prob[b, lanes, :]
            d_probs = nt(dm, cat[b, :, upper])
            delta = jnp.sum(probs * d_probs, axis=1, keepdims=True)
            d_scores = probs * (d_probs - delta)
            d_low = d_scores.astype(BF)
            tall = nn(d_low, cat[b, :, lanes])
            dq_ref[pl.ds(base, PIX), lanes] = (unstacked(tall) * scale).astype(BF)
            d_k = tn(d_low, q)
            d_v = tn(probs.astype(BF), dm)
            for s in range(SLOTS):
                start = pl.multiple_of(near_ref[b * PAD_SLOTS + s] * PIX, PIX)
                acc[pl.ds(start, PIX), lanes] += d_k[s * PIX : (s + 1) * PIX]
                acc[pl.ds(start, PIX), upper] += d_v[s * PIX : (s + 1) * PIX]
            for p in range(PAIRS):
                first = b * PAD_SLOTS + 2 * p
                tile = d_scores[:, p * 2 * PIX : (p + 1) * 2 * PIX]
                tacc[turn_ref[first], lanes, :] += jnp.where(low_half, tile, 0.0)
                tacc[turn_ref[first + 1], lanes, :] += jnp.where(low_half, 0.0, tile)
        return carry

    lax.fori_loop(0, blocks, backward, 0)

    left_ref[...] = acc[:rows, :].astype(BF)
    own_ref[...] = acc[rows : 2 * rows, :]
    right_ref[...] = acc[2 * rows :, :].astype(BF)
    source = lax.broadcasted_iota(jnp.int32, (2 * PIX, PIX), 0) & (PIX - 1)
    target = lax.broadcasted_iota(jnp.int32, (2 * PIX, PIX), 1)
    total = jnp.zeros(bias_ref.shape, F32)
    for turn in range(TURNS):
        pick = (turn_index(source, turn) == target).astype(F32)
        total = total + jnp.dot(tacc[turn], pick, preferred_element_type=F32, precision=HIGH)
    bias_ref[...] = total


def gradient_kernel(
    place_ref,
    x_ref, gain_ref, normed_ref, w_ref, dq_ref, own_ref, fl_ref, fr_ref, dout_ref, mixed_ref,
    dx_ref, gain_out_ref, first_ref, second_ref,
):
    dim = x_ref.shape[1]
    n_member, n_tile, depth, half = first_ref.shape
    x32 = x_ref[...].astype(F32)
    inverse = rms(x32)
    d_kv = own_ref[...] + fl_ref[...].astype(F32) + fr_ref[...].astype(F32)
    d_proj = jnp.concatenate([dq_ref[...], d_kv.astype(BF)], axis=1)
    d_out = dout_ref[...]
    d_normed = nt(d_proj, w_ref[...])
    unit = x32 * inverse
    gain_out_ref[...] = jnp.sum(d_normed * unit, axis=0, keepdims=True)
    d_scaled = d_normed * gain_ref[...]
    inner = jnp.mean(d_scaled * x32, axis=-1, keepdims=True)
    dx_ref[...] = (
        d_out.astype(F32) + inverse * d_scaled - x32 * (inverse * inverse * inverse) * inner
    ).astype(BF)
    d_w = tn(normed_ref[...], d_proj)
    d_o = tn(mixed_ref[...], d_out)
    proj_cols = 3 * dim // n_member
    out_cols = dim // n_member
    for m in range(n_member):
        piece = jnp.concatenate(
            [
                d_w[:, m * proj_cols : (m + 1) * proj_cols],
                d_o[:, m * out_cols : (m + 1) * out_cols],
            ],
            axis=1,
        ).astype(BF)
        to_m = place_ref[0] ^ m
        for t in range(n_tile):
            to_t = place_ref[1] ^ t
            part = piece[t * depth : (t + 1) * depth]
            first_ref[to_m, to_t] = part[:, :half]
            second_ref[to_m, to_t] = part[:, half:]


def call(kernel, outs, n_scalar, n_in, scratch=(), name=None):
    return pl.pallas_call(
        kernel,
        out_shape=outs,
        in_specs=[pl.BlockSpec(memory_space=SM)] * n_scalar
        + [pl.BlockSpec(memory_space=VM)] * n_in,
        out_specs=[pl.BlockSpec(memory_space=VM)] * len(outs),
        scratch_shapes=list(scratch),
        name=name,
    )


def shape(dims, kind):
    return jax.ShapeDtypeStruct(dims, kind)


def swapped(value, axis, bit):
    count = lax.axis_size(axis)
    return lax.ppermute(value, axis, [(i, i ^ bit) for i in range(count)])


def passed_along(value, axis, by):
    count = lax.axis_size(axis)
    pairs = [(i, i + by) for i in range(count) if 0 <= i + by < count]
    return lax.ppermute(value, axis, pairs)


def bits_of(count):
    bits = []
    while (1 << len(bits)) < count:
        bits.append(1 << len(bits))
    return bits


def halved(value, dim):
    size = value.shape[dim] // 2
    keep = lax.slice_in_dim(value, 0, size, axis=dim)
    send = lax.slice_in_dim(value, size, 2 * size, axis=dim)
    return keep, send


def shards(states, teacher, w_qkv, w_out, gain, bias, neighbours, valid, orient):
    x = states[0]
    rows, dim = x.shape
    blocks = neighbours.shape[0]
    heads = bias.shape[0]
    n_tile = lax.axis_size("tile")
    n_member = lax.axis_size("member")
    tile = lax.axis_index("tile")
    member = lax.axis_index("member")
    from_left = passed_along(x, "tile", 1)
    from_right = passed_along(x, "tile", -1)
    near_column = jnp.clip(neighbours // ROWS - tile * COL_DEV + 1, 0, 2)
    near = near_column * ROWS + neighbours % ROWS
    pad = ((0, 0), (0, PAD_SLOTS - SLOTS))
    near = jnp.pad(near, pad).reshape(-1)
    turns = jnp.pad(orient, pad).reshape(-1)
    drop = jnp.pad(jnp.where(valid > 0, 0.0, NEG).astype(F32), pad, constant_values=NEG).reshape(-1)
    gain_row = gain.reshape(1, dim)
    bias_rows = bias.reshape(heads * PIX, PIX)

    normed, proj, table = call(
        own_kernel,
        [
            shape((rows, dim), BF),
            shape((rows, 3 * dim), BF),
            shape((TURNS, heads * PIX, 2 * PIX), F32),
        ],
        0, 4, name="own",
    )(x, gain_row, w_qkv, bias_rows)

    out, d_out, mixed, d_q, d_own, d_left, d_right, bias_term = call(
        attention_kernel,
        [
            shape((rows, dim), BF),
            shape((rows, dim), BF),
            shape((rows, dim), BF),
            shape((rows, dim), BF),
            shape((rows, 2 * dim), F32),
            shape((rows, 2 * dim), BF),
            shape((rows, 2 * dim), BF),
            shape((heads * PIX, PIX), F32),
        ],
        3, 9,
        scratch=[
            pltpu.VMEM((3 * rows, 2 * dim), BF),
            pltpu.VMEM((blocks, PAD_SLOTS * PIX, 2 * dim), BF),
            pltpu.VMEM((blocks, heads * PIX, PAD_SLOTS * PIX), F32),
            pltpu.VMEM((rows, dim), BF),
            pltpu.VMEM((3 * rows, 2 * dim), F32),
            pltpu.VMEM((TURNS, heads * PIX, 2 * PIX), F32),
        ],
        name="attention",
    )(near, turns, drop, x, from_left, from_right, proj, table, gain_row, w_qkv, w_out, teacher)

    back_right = passed_along(d_left, "tile", -1)
    back_left = passed_along(d_right, "tile", 1)

    devices = n_tile * n_member
    both = ("tile", "member")
    spread = bias_term.reshape(devices, heads * PIX * PIX // devices)
    mine = jnp.sum(lax.all_to_all(spread, both, 0, 0, tiled=True), axis=0)
    copies = jnp.broadcast_to(mine[None], (devices,) + mine.shape)
    bias_total = lax.all_to_all(copies, both, 0, 0, tiled=True).reshape(bias.shape)

    depth = dim // n_tile
    place = jnp.stack([member, tile]).astype(jnp.int32)
    piece = shape((n_member, n_tile, depth, dim // 2), BF)
    d_x, gain_term, first, second = call(
        gradient_kernel,
        [shape((rows, dim), BF), shape((1, dim), F32), piece, piece],
        1, 10, name="gradient",
    )(place, x, gain_row, normed, w_qkv, d_q, d_own, back_left, back_right, d_out, mixed)

    gain_copies = jnp.broadcast_to(gain_term, (devices, dim))
    gain_total = jnp.sum(lax.all_to_all(gain_copies, both, 0, 0, tiled=True), axis=0)

    tile_bits = [("tile", bit) for bit in bits_of(n_tile)]
    member_bits = [("member", bit) for bit in bits_of(n_member)]
    near_core, across = member_bits[:1], member_bits[1:]
    first_order = near_core + across + tile_bits
    second_order = near_core + tile_bits[:2] + across + tile_bits[2:]
    done = []
    for value, order in ((first, first_order), (second, second_order)):
        left = {"member": [b for a, b in member_bits], "tile": [b for a, b in tile_bits]}
        for k, (axis, bit) in enumerate(order):
            at = left[axis].index(bit)
            value = reduce_bit(value, axis, bit, at, k == len(order) - 1)
            left[axis].pop(at)
        done.append(value.reshape(depth, dim // 2))
    summed = jnp.concatenate(done, axis=1)
    proj_cols = 3 * dim // n_member
    return (
        out[None],
        d_x[None],
        summed[:, :proj_cols],
        summed[:, proj_cols:],
        gain_total,
        bias_total,
    )


def reduce_bit(value, axis, bit, at, last):
    dim = 0 if axis == "member" else 1
    count = value.shape[dim]
    lead, tail = value.shape[:dim], value.shape[dim + 1 :]
    inner = 1 << at
    split = value.reshape(lead + (count // (2 * inner), 2, inner) + tail)
    keep, send = halved(split, dim + 1)
    total = keep.astype(F32) + swapped(send, axis, bit).astype(F32)
    total = total.reshape(lead + (count // 2,) + tail)
    return total if last else total.astype(BF)


def solution(mesh):
    return jax.shard_map(
        shards,
        mesh=mesh,
        in_specs=(
            P("member", "tile", None),
            P("tile", None),
            P(),
            P(),
            P(),
            P(),
            P("tile", None),
            P("tile", None),
            P("tile", None),
        ),
        out_specs=(
            P("member", "tile", None),
            P("member", "tile", None),
            P("tile", "member"),
            P("tile", "member"),
            P(),
            P(),
        ),
        check_vma=False,
    )
```

time: 503 us -> 124 us (0.25); the launches traced: 497 us -> 124 us
  waiting for transfers between devices: 192 us -> 44.7 us
  local copies, waits for them, and re-layouts: 135 us -> 11.8 us
  matrix products: 66.7 us -> 0 us
  blocking collectives: 39.6 us -> 0 us
  other arithmetic: 33.7 us -> 4.22 us
  Pallas kernels: 0 us -> 27 us
  starting transfers between devices: 15.2 us -> 35 us
  between operations: 15.3 us -> 0.87 us
    psum x1 -> x0, waiting for transfers between devices: 129 us -> none  [shards(): lax.psum((gain_term, bias_term), ('tile', 'member'))]
    dot_general x17 -> x0, matrix products: 66.7 us -> none  [the longest x1 20.5 us: shards(): jnp.einsum('cqmkt,cqmkx->mctx', row_onehot, d_near, precision=HIGH)]
    reshape x16 -> x4, local copies, waits for them, and re-layouts: 66.2 us -> 2.65 us  [the longest x1 0.8 us: shards(): lax.all_to_all(copies, both, 0, 0, tiled=True).reshape(bias.shape)]
    psum x1 -> x0, blocking collectives: 39.6 us -> none  [shards(): lax.psum((gain_term, bias_term), ('tile', 'member'))]
    reduce_scatter x1 -> x0, waiting for transfers between devices: 32.5 us -> none  [shards(): lax.psum_scatter(whole_term.astype(jnp.bfloat16), 'member', scatter_dimen...]
    pallas_call x0 -> x3, Pallas kernels: none -> 27 us  [the longest x1 18.1 us: shards(): call(attention_kernel, [shape((rows, dim), BF), shape((rows, dim), BF), s...]
    unnamed x4 -> x0, waiting for transfers between devices: 15.3 us -> none
    all_to_all x0 -> x3, starting transfers between devices: none -> 14.4 us  [the longest x1 6.07 us: shards(): mine = jnp.sum(lax.all_to_all(spread, both, 0, 0, tiled=True), axis=0)]
  transfers between devices with their start and end apart: 7 -> 17, of which waited for: 5 -> 10; matrix products, arithmetic and copies ran while one was open for 10% -> 10% of each run, Pallas kernels for 0% -> 7%
where the time goes in v1:
time: 124 us
  waiting for transfers between devices  44.7 us (36%)
  starting transfers between devices  35 us (28%)
  Pallas kernels  27 us (22%)
  local copies, waits for them, and re-layouts  11.8 us (10%)
  other arithmetic  4.22 us (3%)
    pallas_call x1, Pallas kernels, shards(): call(attention_kernel, [shape((rows, dim), BF), shape((rows, dim), BF), s...  18.1 us
    ppermute x4, waiting for transfers between devices, passed_along(): return lax.ppermute(value, axis, pairs)  17 us
    ppermute x10, waiting for transfers between devices, swapped(): return lax.ppermute(value, axis, [(i, i ^ bit) for i in range(count)])  14.4 us
    ppermute x4, starting transfers between devices, passed_along(): return lax.ppermute(value, axis, pairs)  12.4 us
    ppermute x10, starting transfers between devices, swapped(): return lax.ppermute(value, axis, [(i, i ^ bit) for i in range(count)])  8.16 us
    all_to_all x1, waiting for transfers between devices, shards(): lax.all_to_all(copies, both, 0, 0, tiled=True).reshape(bias.shape)  7.12 us
    all_to_all x1, waiting for transfers between devices, shards(): lax.all_to_all(gain_copies, both, 0, 0, tiled=True)  6.29 us
    all_to_all x1, starting transfers between devices, shards(): mine = jnp.sum(lax.all_to_all(spread, both, 0, 0, tiled=True), axis=0)  6.07 us
  transfers between devices with their start and end apart: 17, of which 10 were waited for; matrix products, arithmetic and copies ran while one was open for 10% of the time, Pallas kernels for 7%

profile of v1, /device:TPU:0, one launch (start us, length us, event | category | flops | bytes accessed | tf_op | source)
XLA Modules:
  0.0 123.6 jit_solution(2453903283844651224)
XLA Ops:
  0.6 1.3 %collective-permute-start.1 = (bf16[256,512]{1,0:T(8,128)(2,1)}, bf16[256,512]{1,0:T(8,128)(2,1)S(1)}, u32[]{:S(2)}, u32[]{:S(2)}) collective-permute-start(bf16[256,512]{1,0:T(8,128)(2,1)} %bitcast.44), channel_id=1, source_target_pairs={{4,0},{8,4},{12,8},{16,12},{20,16},{24,20},{28,24},{5,1},{9,5},{13... | collective-permute-start | bytes 786440 | tf_op jit(solution)/shard_map/ppermute | solution.py:241
  1.9 5.5 %collective-permute-start = (bf16[256,512]{1,0:T(8,128)(2,1)}, bf16[256,512]{1,0:T(8,128)(2,1)S(1)}, u32[]{:S(2)}, u32[]{:S(2)}) collective-permute-start(bf16[256,512]{1,0:T(8,128)(2,1)} %bitcast.45), channel_id=1, source_target_pairs={{0,4},{4,8},{8,12},{12,16},{16,20},{20,24},{24,28},{1,5},{5,9},{9,... | collective-permute-start | bytes 786440 | tf_op jit(solution)/shard_map/ppermute | solution.py:241
  11.4 4.0 %own.1 = (bf16[256,512]{1,0:T(8,128)(2,1)}, bf16[256,1536]{1,0:T(8,128)(2,1)}, f32[4,512,128]{2,1,0:T(8,128)}) custom-call(bf16[256,512]{1,0:T(8,128)(2,1)} %bitcast.46, f32[1,512]{1,0:T(1,128)} %bitcast.62, bf16[512,1536]{1,0:T(8,128)(2,1)} %w_ref.5, f32[512,64]{1,0:T(8,128)} %bitcast.61), custom_call_target="tpu_custom_call" | custom-call | tf_op jit(solution)/shard_map/own/pallas_call | solution.py:278
  15.4 2.5 %collective-permute-done.xl_ref = bf16[256,512]{1,0:T(8,128)(2,1)S(1)} collective-permute-done((bf16[256,512]{1,0:T(8,128)(2,1)}, bf16[256,512]{1,0:T(8,128)(2,1)S(1)}, u32[]{:S(2)}, u32[]{:S(2)}) %collective-permute-start) | collective-permute-done | bytes 262176 | tf_op jit(solution)/shard_map/ppermute | solution.py:241
  18.6 18.1 %attention.1 = (bf16[256,512]{1,0:T(8,128)(2,1)}, bf16[256,512]{1,0:T(8,128)(2,1)}, bf16[256,512]{1,0:T(8,128)(2,1)}, bf16[256,512]{1,0:T(8,128)(2,1)}, f32[256,...) custom-call(s32[40]{0:T(128)} %reshape.169.near_ref, ...), custom_call_target="tpu_custom_call" | custom-call | tf_op jit(solution)/shard_map/attention/pallas_call | solution.py:288
  36.7 4.3 %collective-permute-start.2 = (bf16[256,1024]{1,0:T(8,128)(2,1)}, bf16[256,1024]{1,0:T(8,128)(2,1)S(1)}, u32[]{:S(2)}, u32[]{:S(2)}) collective-permute-start(bf16[256,1024]{1,0:T(8,128)(2,1)} %get-tuple-element.27), channel_id=1, source_target_pairs={{0,4},{4,8},{8,12},{12,16},{16,20},{20,24},{24,28},{1,5},{5,9},{9,... | collective-permute-start | bytes 1572872 | tf_op jit(solution)/shard_map/ppermute | solution.py:241
  41.0 1.3 %collective-permute-start.3 = (bf16[256,1024]{1,0:T(8,128)(2,1)}, bf16[256,1024]{1,0:T(8,128)(2,1)S(1)}, u32[]{:S(2)}, u32[]{:S(2)}) collective-permute-start(bf16[256,1024]{1,0:T(8,128)(2,1)} %get-tuple-element.28), channel_id=1, source_target_pairs={{4,0},{8,4},{12,8},{16,12},{20,16},{24,20},{28,24},{5,1},{9,5},{13... | collective-permute-start | bytes 1572872 | tf_op jit(solution)/shard_map/ppermute | solution.py:241
  42.9 1.8 %all_to_all.18 = f32[32,1,1024]{2,1,0:T(1,128)} reshape(f32[512,64]{1,0:T(8,128)} %get-tuple-element.35) | data formatting | bytes 262144 | tf_op jit(solution)/shard_map/all_to_all | solution.py:318
  44.7 6.1 %all-to-all-start.1 = ((f32[32,1,1024]{2,1,0:T(1,128)}), f32[32,1,1024]{2,1,0:T(1,128)S(1)}, u32[]{:S(2)}, u32[]{:S(2)}) async-start(f32[32,1,1024]{2,1,0:T(1,128)} %all_to_all.18), calls=%async_computation.1 | async-start | bytes 262144 | tf_op jit(solution)/shard_map/all_to_all | solution.py:318
  50.8 14.4 %collective-permute-done.2.fl_ref = bf16[256,1024]{1,0:T(8,128)(2,1)S(1)} collective-permute-done((bf16[256,1024]{1,0:T(8,128)(2,1)}, bf16[256,1024]{1,0:T(8,128)(2,1)S(1)}, u32[]{:S(2)}, u32[]{:S(2)}) %collective-permute-start.2) | collective-permute-done | bytes 524320 | tf_op jit(solution)/shard_map/ppermute | solution.py:241
  66.2 5.0 %gradient.1 = (bf16[256,512]{1,0:T(8,128)(2,1)}, f32[1,512]{1,0:T(1,128)}, bf16[4,8,64,256]{3,2,1,0:T(8,128)(2,1)}, bf16[4,8,64,256]{3,2,1,0:T(8,128)(2,1)}) custom-call(s32[2]{0:T(128)} %pad_add_fusion.place_ref, bf16[256,512]{1,0:T(8,128)(2,1)} %bitcast.48, f32[1,512]{1,0:T(1,128)} %bitcast.64, bf16[256,512]{1,0:T(8,128)(2,1)} %get-tuple-element.24.normed_ref, ...), custom_call_target="tpu_custom_call" | custom-call | tf_op jit(solution)/shard_map/gradient/pallas_call | solution.py:325
  71.1 2.0 %slice_bitcast_fusion = bf16[2,1,1,8,64,256]{5,4,3,0,2,1:T(8,128)(2,1)} fusion(bf16[2,2,1,8,64,256]{5,4,3,1,0,2:T(8,128)(2,1)} %bitcast.57), kind=kLoop, calls=%fused_computation.3 | loop fusion | bytes 1048576
  74.0 5.8 %all-to-all-start.2 = ((f32[32,1,1024]{2,1,0:T(1,128)}), f32[32,1,1024]{2,1,0:T(1,128)S(1)}, u32[]{:S(2)}, u32[]{:S(2)}) async-start(f32[32,1,1024]{2,1,0:T(1,128)} %broadcast_in_dim.30), calls=%async_computation.2 | async-start | bytes 262144 | tf_op jit(solution)/shard_map/all_to_all | solution.py:320
  79.8 0.8 slice_bitcast_fusion.2
  80.9 7.1 %all-to-all-done.2 = f32[32,1,1024]{2,1,0:T(1,128)S(1)} async-done(((f32[32,1,1024]{2,1,0:T(1,128)}), f32[32,1,1024]{2,1,0:T(1,128)S(1)}, u32[]{:S(2)}, u32[]{:S(2)}) %all-to-all-start.2) | async-done | bytes 131104 | tf_op jit(solution)/shard_map/all_to_all | solution.py:320
  88.7 2.6 %all-to-all-start = ((f32[32,1,512]{2,1,0:T(1,128)}), f32[32,1,512]{2,1,0:T(1,128)S(1)}, u32[]{:S(2)}, u32[]{:S(2)}) async-start(f32[32,1,512]{2,1,0:T(1,128)} %broadcast_in_dim.29), calls=%async_computation | async-start | bytes 131072 | tf_op jit(solution)/shard_map/all_to_all | solution.py:332
  92.4 6.3 %all-to-all-done = f32[32,1,512]{2,1,0:T(1,128)S(1)} async-done(((f32[32,1,512]{2,1,0:T(1,128)}), f32[32,1,512]{2,1,0:T(1,128)S(1)}, u32[]{:S(2)}, u32[]{:S(2)}) %all-to-all-start) | async-done | bytes 65568 | tf_op jit(solution)/shard_map/all_to_all | solution.py:332
  101.1 6.8 %collective-permute-done.10 = bf16[2,4,1,1,64,256]{5,4,2,1,0,3:T(8,128)(2,1)S(1)} collective-permute-done((bf16[2,4,1,1,64,256]{5,4,2,1,0,3:T(8,128)(2,1)S(1)}, bf16[2,4,1,1,64,256]{5,4,2,1,0,3:T(8,128)(2,1)S(1)}, u32[]{:S(2)}, u32[]{:S(2)}) %collective-permute-start.10) | collective-permute-done | bytes 262176 | tf_op jit(solution)/shard_map/ppermute | solution.py:235
  108.5 1.6 %collective-permute-start.6 = (bf16[1,4,1,1,64,256]{5,4,2,1,3,0:T(8,128)(2,1)S(1)}, bf16[1,4,1,1,64,256]{5,4,2,1,3,0:T(8,128)(2,1)S(1)}, u32[]{:S(2)}, u32[]{:S(2)}) collective-permute-start(bf16[1,4,1,1,64,256]{5,4,2,1,3,0:T(8,128)(2,1)S(1)} %slice.93), channel_id=1, source_target_pairs={{0,4},{4,0},{8,12},{12,8},{16,20},{20,16},{24,28},{28,24},{1,5},{5... | collective-permute-start | bytes 393224 | tf_op jit(solution)/shard_map/ppermute | solution.py:235
  110.1 3.0 %collective-permute-done.11 = bf16[2,2,1,1,64,256]{5,4,1,0,3,2:T(8,128)(2,1)S(1)} collective-permute-done((bf16[2,2,1,1,64,256]{5,4,1,0,3,2:T(8,128)(2,1)S(1)}, bf16[2,2,1,1,64,256]{5,4,1,0,3,2:T(8,128)(2,1)S(1)}, u32[]{:S(2)}, u32[]{:S(2)}) %collective-permute-start.11) | collective-permute-done | bytes 131104 | tf_op jit(solution)/shard_map/ppermute | solution.py:235
  113.6 1.7 %collective-permute-start.7 = (bf16[1,2,1,1,64,256]{5,4,2,1,3,0:T(8,128)(2,1)S(1)}, bf16[1,2,1,1,64,256]{5,4,2,1,3,0:T(8,128)(2,1)S(1)}, u32[]{:S(2)}, u32[]{:S(2)}) collective-permute-start(bf16[1,2,1,1,64,256]{5,4,2,1,3,0:T(8,128)(2,1)S(1)} %slice.95), channel_id=1, source_target_pairs={{0,8},{4,12},{8,0},{12,4},{16,24},{20,28},{24,16},{28,20},{1,9},{5... | collective-permute-start | bytes 196616 | tf_op jit(solution)/shard_map/ppermute | solution.py:235
  115.3 2.1 %collective-permute-done.12 = bf16[1,1,1,2,64,256]{5,4,3,2,1,0:T(8,128)(2,1)S(1)} collective-permute-done((bf16[1,1,1,2,64,256]{5,4,3,2,1,0:T(8,128)(2,1)S(1)}, bf16[1,1,1,2,64,256]{5,4,3,2,1,0:T(8,128)(2,1)S(1)}, u32[]{:S(2)}, u32[]{:S(2)}) %collective-permute-start.12) | collective-permute-done | bytes 65568 | tf_op jit(solution)/shard_map/ppermute | solution.py:235
  118.0 2.5 %collective-permute-start.8 = (bf16[1,1,1,1,64,256]{5,4,2,3,1,0:T(8,128)(2,1)S(1)}, bf16[1,1,1,1,64,256]{5,4,2,3,1,0:T(8,128)(2,1)S(1)}, u32[]{:S(2)}, u32[]{:S(2)}) collective-permute-start(bf16[1,1,1,1,64,256]{5,4,2,3,1,0:T(8,128)(2,1)S(1)} %slice.97), channel_id=1, source_target_pairs={{0,16},{4,20},{8,24},{12,28},{16,0},{20,4},{24,8},{28,12},{1,17},{... | collective-permute-start | bytes 98312 | tf_op jit(solution)/shard_map/ppermute | solution.py:235
  120.5 1.8 %collective-permute-done.13 = bf16[1,1,1,1,64,256]{5,4,3,2,1,0:T(8,128)(2,1)S(1)} collective-permute-done((bf16[1,1,1,1,64,256]{5,4,3,2,1,0:T(8,128)(2,1)S(1)}, bf16[1,1,1,1,64,256]{5,4,3,2,1,0:T(8,128)(2,1)S(1)}, u32[]{:S(2)}, u32[]{:S(2)}) %collective-permute-start.13) | collective-permute-done | bytes 32800 | tf_op jit(solution)/shard_map/ppermute | solution.py:235
  (65 shorter events, 14.5 us)
Async XLA Ops:
  0.6 14.8 %collective-permute-start.1 = (bf16[256,512]{1,0:T(8,128)(2,1)}, bf16[256,512]{1,0:T(8,128)(2,1)S(1)}, u32[]{:S(2)}, u32[]{:S(2)}) collective-permute-start(bf16[256,512]{1,0:T(8,128)(2,1)} %bitcast.44), channel_id=1, source_target_pairs={{4,0},{8,4},{12,8},{16,12},{20,16},{24,20},{28,24},{5,1},{9,5},{13... | collective-permute-start | bytes 786440 | tf_op jit(solution)/shard_map/ppermute | solution.py:241
  1.9 16.0 %collective-permute-start = (bf16[256,512]{1,0:T(8,128)(2,1)}, bf16[256,512]{1,0:T(8,128)(2,1)S(1)}, u32[]{:S(2)}, u32[]{:S(2)}) collective-permute-start(bf16[256,512]{1,0:T(8,128)(2,1)} %bitcast.45), channel_id=1, source_target_pairs={{0,4},{4,8},{8,12},{12,16},{16,20},{20,24},{24,28},{1,5},{5,9},{9,... | collective-permute-start | bytes 786440 | tf_op jit(solution)/shard_map/ppermute | solution.py:241
  15.4 2.5 %copy-start.4 = (bf16[256,512]{1,0:T(8,128)(2,1)}, bf16[256,512]{1,0:T(8,128)(2,1)S(1)}, u32[]{:S(2)}) copy-start(bf16[256,512]{1,0:T(8,128)(2,1)S(1)} %collective-permute-done.1.xr_ref) | copy-start | bytes 786436
  17.9 0.7 copy-start.5
  36.7 28.5 %collective-permute-start.2 = (bf16[256,1024]{1,0:T(8,128)(2,1)}, bf16[256,1024]{1,0:T(8,128)(2,1)S(1)}, u32[]{:S(2)}, u32[]{:S(2)}) collective-permute-start(bf16[256,1024]{1,0:T(8,128)(2,1)} %get-tuple-element.27), channel_id=1, source_target_pairs={{0,4},{4,8},{8,12},{12,16},{16,20},{20,24},{24,28},{1,5},{5,9},{9,... | collective-permute-start | bytes 1572872 | tf_op jit(solution)/shard_map/ppermute | solution.py:241
  41.0 24.2 %collective-permute-start.3 = (bf16[256,1024]{1,0:T(8,128)(2,1)}, bf16[256,1024]{1,0:T(8,128)(2,1)S(1)}, u32[]{:S(2)}, u32[]{:S(2)}) collective-permute-start(bf16[256,1024]{1,0:T(8,128)(2,1)} %get-tuple-element.28), channel_id=1, source_target_pairs={{4,0},{8,4},{12,8},{16,12},{20,16},{24,20},{28,24},{5,1},{9,5},{13... | collective-permute-start | bytes 1572872 | tf_op jit(solution)/shard_map/ppermute | solution.py:241
  44.7 28.5 %all-to-all-start.1 = ((f32[32,1,1024]{2,1,0:T(1,128)}), f32[32,1,1024]{2,1,0:T(1,128)S(1)}, u32[]{:S(2)}, u32[]{:S(2)}) async-start(f32[32,1,1024]{2,1,0:T(1,128)} %all_to_all.18), calls=%async_computation.1 | async-start | bytes 262144 | tf_op jit(solution)/shard_map/all_to_all | solution.py:318
  65.2 0.8 copy-start.2
  65.2 1.0 copy-start.3
  71.1 8.7 %copy-start = (bf16[4,8,64,256]{3,2,1,0:T(8,128)(2,1)S(1)}, bf16[4,8,64,256]{3,2,1,0:T(8,128)(2,1)}, u32[]{:S(2)}) copy-start(bf16[4,8,64,256]{3,2,1,0:T(8,128)(2,1)} %get-tuple-element.32) | copy-start | bytes 3145732
  71.1 16.9 %copy-start.6 = (f32[1,512]{1,0:T(1,128)S(1)}, f32[1,512]{1,0:T(1,128)}, u32[]{:S(2)}) copy-start(f32[1,512]{1,0:T(1,128)} %get-tuple-element.34) | copy-start | bytes 6148
  71.1 28.2 %copy-start.1 = (bf16[4,8,64,256]{3,2,1,0:T(8,128)(2,1)S(1)}, bf16[4,8,64,256]{3,2,1,0:T(8,128)(2,1)}, u32[]{:S(2)}) copy-start(bf16[4,8,64,256]{3,2,1,0:T(8,128)(2,1)} %get-tuple-element.33) | copy-start | bytes 3145732
  73.2 26.1 %collective-permute-start.9 = (bf16[2,1,1,8,64,256]{5,4,3,0,2,1:T(8,128)(2,1)}, bf16[2,1,1,8,64,256]{5,4,3,0,2,1:T(8,128)(2,1)S(1)}, u32[]{:S(2)}, u32[]{:S(2)}) collective-permute-start(bf16[2,1,1,8,64,256]{5,4,3,0,2,1:T(8,128)(2,1)} %slice_bitcast_fusion), channel_id=1, source_target_pairs={{0,1},{1,0},{2,3},{3,2},{4,5},{5,4},{6,7},{7,6},{8,9},{9,8},{10,11... | collective-permute-start | bytes 1572872 | tf_op jit(solution)/shard_map/ppermute | solution.py:235
  74.0 14.0 %all-to-all-start.2 = ((f32[32,1,1024]{2,1,0:T(1,128)}), f32[32,1,1024]{2,1,0:T(1,128)S(1)}, u32[]{:S(2)}, u32[]{:S(2)}) async-start(f32[32,1,1024]{2,1,0:T(1,128)} %broadcast_in_dim.30), calls=%async_computation.2 | async-start | bytes 262144 | tf_op jit(solution)/shard_map/all_to_all | solution.py:320
  80.7 19.5 %collective-permute-start.4 = (bf16[2,1,1,8,64,256]{5,4,3,0,2,1:T(8,128)(2,1)}, bf16[2,1,1,8,64,256]{5,4,3,0,2,1:T(8,128)(2,1)S(1)}, u32[]{:S(2)}, u32[]{:S(2)}) collective-permute-start(bf16[2,1,1,8,64,256]{5,4,3,0,2,1:T(8,128)(2,1)} %slice_bitcast_fusion.2), channel_id=1, source_target_pairs={{0,1},{1,0},{2,3},{3,2},{4,5},{5,4},{6,7},{7,6},{8,9},{9,8},{10,11... | collective-permute-start | bytes 1572872 | tf_op jit(solution)/shard_map/ppermute | solution.py:235
  88.7 10.0 %all-to-all-start = ((f32[32,1,512]{2,1,0:T(1,128)}), f32[32,1,512]{2,1,0:T(1,128)S(1)}, u32[]{:S(2)}, u32[]{:S(2)}) async-start(f32[32,1,512]{2,1,0:T(1,128)} %broadcast_in_dim.29), calls=%async_computation | async-start | bytes 131072 | tf_op jit(solution)/shard_map/all_to_all | solution.py:332
  99.5 8.4 %collective-permute-start.10 = (bf16[2,4,1,1,64,256]{5,4,2,1,0,3:T(8,128)(2,1)S(1)}, bf16[2,4,1,1,64,256]{5,4,2,1,0,3:T(8,128)(2,1)S(1)}, u32[]{:S(2)}, u32[]{:S(2)}) collective-permute-start(bf16[2,4,1,1,64,256]{5,4,2,1,0,3:T(8,128)(2,1)S(1)} %slice.101), channel_id=1, source_target_pairs={{0,4},{4,0},{8,12},{12,8},{16,20},{20,16},{24,28},{28,24},{1,5},{5... | collective-permute-start | bytes 786440 | tf_op jit(solution)/shard_map/ppermute | solution.py:235
  100.4 8.0 %collective-permute-start.5 = (bf16[1,1,1,8,64,256]{5,4,3,2,1,0:T(8,128)(2,1)S(1)}, bf16[1,1,1,8,64,256]{5,4,3,2,1,0:T(8,128)(2,1)S(1)}, u32[]{:S(2)}, u32[]{:S(2)}) collective-permute-start(bf16[1,1,1,8,64,256]{5,4,3,2,1,0:T(8,128)(2,1)S(1)} %slice.91), channel_id=1, source_target_pairs={{0,2},{1,3},{2,0},{3,1},{4,6},{5,7},{6,4},{7,5},{8,10},{9,11},{10,... | collective-permute-start | bytes 786440 | tf_op jit(solution)/shard_map/ppermute | solution.py:235
  108.0 5.0 %collective-permute-start.11 = (bf16[2,2,1,1,64,256]{5,4,1,0,3,2:T(8,128)(2,1)S(1)}, bf16[2,2,1,1,64,256]{5,4,1,0,3,2:T(8,128)(2,1)S(1)}, u32[]{:S(2)}, u32[]{:S(2)}) collective-permute-start(bf16[2,2,1,1,64,256]{5,4,1,0,3,2:T(8,128)(2,1)S(1)} %slice_bitcast_fusion.4), channel_id=1, source_target_pairs={{0,8},{4,12},{8,0},{12,4},{16,24},{20,28},{24,16},{28,20},{1,9},{5... | collective-permute-start | bytes 393224 | tf_op jit(solution)/shard_map/ppermute | solution.py:235
  108.5 5.1 %collective-permute-start.6 = (bf16[1,4,1,1,64,256]{5,4,2,1,3,0:T(8,128)(2,1)S(1)}, bf16[1,4,1,1,64,256]{5,4,2,1,3,0:T(8,128)(2,1)S(1)}, u32[]{:S(2)}, u32[]{:S(2)}) collective-permute-start(bf16[1,4,1,1,64,256]{5,4,2,1,3,0:T(8,128)(2,1)S(1)} %slice.93), channel_id=1, source_target_pairs={{0,4},{4,0},{8,12},{12,8},{16,20},{20,16},{24,28},{28,24},{1,5},{5... | collective-permute-start | bytes 393224 | tf_op jit(solution)/shard_map/ppermute | solution.py:235
  113.1 4.3 %collective-permute-start.12 = (bf16[1,1,1,2,64,256]{5,4,3,2,1,0:T(8,128)(2,1)S(1)}, bf16[1,1,1,2,64,256]{5,4,3,2,1,0:T(8,128)(2,1)S(1)}, u32[]{:S(2)}, u32[]{:S(2)}) collective-permute-start(bf16[1,1,1,2,64,256]{5,4,3,2,1,0:T(8,128)(2,1)S(1)} %slice.105), channel_id=1, source_target_pairs={{0,2},{1,3},{2,0},{3,1},{4,6},{5,7},{6,4},{7,5},{8,10},{9,11},{10,... | collective-permute-start | bytes 196616 | tf_op jit(solution)/shard_map/ppermute | solution.py:235
  113.6 4.3 %collective-permute-start.7 = (bf16[1,2,1,1,64,256]{5,4,2,1,3,0:T(8,128)(2,1)S(1)}, bf16[1,2,1,1,64,256]{5,4,2,1,3,0:T(8,128)(2,1)S(1)}, u32[]{:S(2)}, u32[]{:S(2)}) collective-permute-start(bf16[1,2,1,1,64,256]{5,4,2,1,3,0:T(8,128)(2,1)S(1)} %slice.95), channel_id=1, source_target_pairs={{0,8},{4,12},{8,0},{12,4},{16,24},{20,28},{24,16},{28,20},{1,9},{5... | collective-permute-start | bytes 196616 | tf_op jit(solution)/shard_map/ppermute | solution.py:235
  117.4 4.9 %collective-permute-start.13 = (bf16[1,1,1,1,64,256]{5,4,3,2,1,0:T(8,128)(2,1)S(1)}, bf16[1,1,1,1,64,256]{5,4,3,2,1,0:T(8,128)(2,1)S(1)}, u32[]{:S(2)}, u32[]{:S(2)}) collective-permute-start(bf16[1,1,1,1,64,256]{5,4,3,2,1,0:T(8,128)(2,1)S(1)} %slice.107), channel_id=1, source_target_pairs={{0,16},{4,20},{8,24},{12,28},{16,0},{20,4},{24,8},{28,12},{1,17},{... | collective-permute-start | bytes 98312 | tf_op jit(solution)/shard_map/ppermute | solution.py:235
  118.0 5.0 %collective-permute-start.8 = (bf16[1,1,1,1,64,256]{5,4,2,3,1,0:T(8,128)(2,1)S(1)}, bf16[1,1,1,1,64,256]{5,4,2,3,1,0:T(8,128)(2,1)S(1)}, u32[]{:S(2)}, u32[]{:S(2)}) collective-permute-start(bf16[1,1,1,1,64,256]{5,4,2,3,1,0:T(8,128)(2,1)S(1)} %slice.97), channel_id=1, source_target_pairs={{0,16},{4,20},{8,24},{12,28},{16,0},{20,4},{24,8},{28,12},{1,17},{... | collective-permute-start | bytes 98312 | tf_op jit(solution)/shard_map/ppermute | solution.py:235
